TPU v7x, 32 devices: a whole 2x2x4 slice. The times are simulated.
32 devices in a mesh: macro: 4 (over y, x), micro: 8 (over z, core).
Axes of the slice: x: 2, y: 2, z: 4, core: 2. Of those that a mesh axis runs over, the one named last changes fastest.
Arguments:
- displacement: float32 [3, 8, 16, 256], P(None, 'macro', 'micro'), may hold values from -6 to 6
- load: float32 [3, 8, 16, 256], P(None, 'macro', 'micro'), may hold values from -6 to 6
- routes: int32 [4, 8, 1024, 1], P('macro', 'micro'), may hold values from 0 to 7; in each aligned block of 1024 rows (0 to 1023, 1024 to 2047, ..., all dimensions but the last counted through in order) at most 256 rows name the same one
- counts: int32 [4, 8, 1024], P('macro', 'micro'), may hold values from 1 to 4
- stiffness: bfloat16 [8, 512, 512], P('micro'), may hold values from -0.5 to 2.5, as said below
- precond: bfloat16 [8, 512, 512], P('micro'), may hold values from -0.5 to 2.5, as said below
- forcing: bfloat16 [8, 6, 512], P('micro'), may hold values from -2.5 to 2.5
- coupling: bfloat16 [8, 512, 6], P('micro'), may hold values from -0.25 to 0.25
- lame_first: float32 [8], P('micro'), may hold values from 0.5 to 2
- lame_shear: float32 [8], P('micro'), may hold values from 0.5 to 2
Outputs:
- increment: float32 [3, 8, 16, 256], P(None, 'macro', 'micro')
- residual: float32 [3, 8, 16, 256], P(None, 'macro', 'micro')
Inputs may be any that keep to these rules, and one draw needn't show every extreme that they name: `routes`: among the points of one block (one device's points), no owner is named by more than 256 points, a bound that some block reaches. `stiffness`: Symmetric. `precond`: Symmetric.
All inputs are finite; a program needn't handle non-finite values.
Results may differ from a plain program's by a relative error of at most 0.002.
Values sent between devices are 32-bit elements; how exact they have to be, the bound alone decides.
A program may use at most 64 MiB of HBM per device.

v0:
```python
import jax
import jax.numpy as jnp
from jax import lax
from jax.sharding import PartitionSpec as P

ITMAX = 4
ITERS = 5
BETA = 0.1
OMEGA = 0.8
MASS = 0.1
VOIGT = ((0, 5, 4), (5, 1, 3), (4, 3, 2))
ALL_PAIRS = tuple(
    ((first_axis, second_axis) for first_axis in range(6) for second_axis in range(6))
)


def with_halo(block, sides, width):
    for axis, dim in sides:
        count = lax.axis_size(axis)
        forward = [(i, i + 1) for i in range(count - 1)]
        backward = [(target, source) for source, target in forward]
        low = lax.ppermute(
            lax.slice_in_dim(block, block.shape[dim] - width, None, axis=dim), axis, forward
        )
        high = lax.ppermute(lax.slice_in_dim(block, 0, width, axis=dim), axis, backward)
        block = jnp.concatenate([low, block, high], axis=dim)
    return block


def passed_along(value, axis, steps):
    count = lax.axis_size(axis)
    initial, last = (max(0, -steps), min(count, count - steps))
    return lax.ppermute(value, axis, [(source, source + steps) for source in range(initial, last)])


def element_strain(nodes):
    count_x = nodes.shape[1] - 1
    count_y = nodes.shape[2] - 1
    count_z = nodes.shape[3]
    padded = jnp.pad(nodes, ((0, 0), (0, 0), (0, 0), (0, 1)))
    zeros = jnp.zeros((3, count_x, count_y, count_z), jnp.float32)
    grad_x, grad_y, grad_z = (zeros, zeros, zeros)
    for corner_x in (0, 1):
        for corner_y in (0, 1):
            for corner_z in (0, 1):
                piece = padded[
                    :,
                    corner_x : corner_x + count_x,
                    corner_y : corner_y + count_y,
                    corner_z : corner_z + count_z,
                ]
                grad_x = grad_x + 0.25 * (2 * corner_x - 1) * piece
                grad_y = grad_y + 0.25 * (2 * corner_y - 1) * piece
                grad_z = grad_z + 0.25 * (2 * corner_z - 1) * piece
    return jnp.stack(
        [
            grad_x[0],
            grad_y[1],
            grad_z[2],
            grad_z[1] + grad_y[2],
            grad_z[0] + grad_x[2],
            grad_y[0] + grad_x[1],
        ]
    )


def node_force(stress):
    count_x, count_y, count_z = (stress.shape[1], stress.shape[2], stress.shape[3])
    forces = jnp.zeros((3, count_x + 1, count_y + 1, count_z + 1), jnp.float32)
    for corner_x in (0, 1):
        for corner_y in (0, 1):
            for corner_z in (0, 1):
                signs = (2 * corner_x - 1, 2 * corner_y - 1, 2 * corner_z - 1)
                parts = []
                for component in range(3):
                    table = VOIGT[component]
                    parts.append(
                        0.25
                        * (
                            signs[0] * stress[table[0]]
                            + signs[1] * stress[table[1]]
                            + signs[2] * stress[table[2]]
                        )
                    )
                contrib = jnp.stack(parts)
                forces = forces + jnp.pad(
                    contrib,
                    (
                        (0, 0),
                        (corner_x, 1 - corner_x),
                        (corner_y, 1 - corner_y),
                        (corner_z, 1 - corner_z),
                    ),
                )
    return forces


def micro_solve(
    strain, sweeps, stiffness, precond, forcing, coupling, lame_first, lame_shear, pairs
):
    strain_half = strain.astype(jnp.bfloat16)
    modal_load = lax.dot_general(
        strain_half, forcing, (((0,), (0,)), ((), ())), preferred_element_type=jnp.float32
    )
    modes = jnp.zeros_like(modal_load)
    for sweep in range(ITMAX):
        misfit = (
            jnp.dot(modes.astype(jnp.bfloat16), stiffness, preferred_element_type=jnp.float32)
            + BETA * jnp.tanh(modes)
            - modal_load
        )
        update = modes - OMEGA * jnp.dot(
            misfit.astype(jnp.bfloat16), precond, preferred_element_type=jnp.float32
        )
        modes = jnp.where((sweeps[0] > sweep)[:, None], update, modes)
    trace = strain[0] + strain[1] + strain[2]
    elastic = jnp.stack(
        [
            lame_first * trace + 2.0 * lame_shear * strain[0],
            lame_first * trace + 2.0 * lame_shear * strain[1],
            lame_first * trace + 2.0 * lame_shear * strain[2],
            lame_shear * strain[3],
            lame_shear * strain[4],
            lame_shear * strain[5],
        ]
    )
    stress = elastic + lax.dot_general(
        coupling,
        modes.astype(jnp.bfloat16),
        (((0,), (1,)), ((), ())),
        preferred_element_type=jnp.float32,
    )
    slope = 1.0 - jnp.tanh(modes) ** 2
    wide = coupling.astype(jnp.float32)
    products = jnp.stack([wide[:, pair[0]] * wide[:, pair[1]] for pair in pairs], axis=1)
    extra = lax.dot_general(
        products,
        slope,
        (((0,), (1,)), ((), ())),
        precision=lax.Precision.HIGHEST,
        preferred_element_type=jnp.float32,
    )
    base = jnp.stack(
        [
            lame_first * float(pair[0] < 3 and pair[1] < 3)
            + lame_shear
            * (
                2.0 * float(pair[0] == pair[1] and pair[0] < 3)
                + float(pair[0] == pair[1] and pair[0] >= 3)
            )
            for pair in pairs
        ]
    )
    return jnp.concatenate([stress, extra + base[:, None]], axis=0)


def extend(field):
    return with_halo(field, (("macro", 1), ("micro", 2)), 1)


def operate(field, tangent_ext):
    strain = element_strain(extend(field))
    stress = jnp.sum(tangent_ext * strain[None], axis=1)
    return MASS * field + node_force(stress)[:, 1:-1, 1:-1, :-1]


def two_products(residual, image):
    return lax.psum((jnp.sum(residual * residual), jnp.sum(residual * image)), ("macro", "micro"))


def shards(
    displacement,
    load,
    routes,
    counts,
    stiffness,
    precond,
    forcing,
    coupling,
    lame_first,
    lame_shear,
):
    count_x, count_y, count_z = (
        displacement.shape[1],
        displacement.shape[2],
        displacement.shape[3],
    )
    points = count_x * count_y * count_z
    owners = lax.axis_size("micro")
    capacity = max(2, 2 * points // owners)
    strain_ext = element_strain(extend(displacement))
    strain_points = strain_ext[:, 1:, 1:].reshape(6, points)
    owner_of = routes.reshape(points)
    sweeps_of = counts.reshape(points)
    onehot = (owner_of[:, None] == jnp.arange(owners, dtype=jnp.int32)[None, :]).astype(jnp.int32)
    ranks = jnp.sum((jnp.cumsum(onehot, axis=0) - 1) * onehot, axis=1)
    target = owner_of * capacity + ranks
    send_strain = jnp.zeros((6, owners * capacity), jnp.float32).at[:, target].set(strain_points)
    send_sweeps = jnp.zeros((1, owners * capacity), jnp.int32).at[0, target].set(sweeps_of)
    got_strain, got_sweeps = (
        lax.all_to_all(send_strain, "micro", split_axis=1, concat_axis=1, tiled=True),
        lax.all_to_all(send_sweeps, "micro", split_axis=1, concat_axis=1, tiled=True),
    )
    rows = micro_solve(
        got_strain,
        got_sweeps,
        stiffness[0],
        precond[0],
        forcing[0],
        coupling[0],
        lame_first[0],
        lame_shear[0],
        ALL_PAIRS,
    )
    back = lax.all_to_all(rows, "micro", split_axis=1, concat_axis=1, tiled=True)
    values = jnp.take(back, target, axis=1)
    values = values.reshape(42, count_x, count_y, count_z)
    left_x = passed_along(values[:, -1:], "macro", 1)
    values = jnp.concatenate([left_x, values], axis=1)
    left_y = passed_along(values[:, :, -1:], "micro", 1)
    values = jnp.concatenate([left_y, values], axis=2)
    stress_ext = values[:6]
    tangent_ext = values[6:].reshape(6, 6, count_x + 1, count_y + 1, count_z)
    rhs = load - node_force(stress_ext)[:, 1:-1, 1:-1, :-1]

    def apply(field):
        return operate(field, tangent_ext)

    increment = jnp.zeros_like(rhs)
    residual = rhs
    image = apply(residual)
    norm_now, product = two_products(residual, image)
    alpha = norm_now / product
    direction, along = (residual, image)
    for step in range(ITERS):
        increment = increment + alpha * direction
        residual = residual - alpha * along
        if step + 1 < ITERS:
            image = apply(residual)
            norm_next, product = two_products(residual, image)
            ratio = norm_next / norm_now
            alpha = norm_next / (product - ratio * norm_next / alpha)
            direction = residual + ratio * direction
            along = image + ratio * along
            norm_now = norm_next
    return (increment, residual)


def solution(mesh):
    in_specs = (
        P(None, "macro", "micro", None),
        P(None, "macro", "micro", None),
        P("macro", "micro", None, None),
        P("macro", "micro", None),
        P("micro", None, None),
        P("micro", None, None),
        P("micro", None, None),
        P("micro", None, None),
        P("micro"),
        P("micro"),
    )
    out_specs = (P(None, "macro", "micro", None), P(None, "macro", "micro", None))
    return jax.shard_map(shards, mesh=mesh, in_specs=in_specs, out_specs=out_specs, check_vma=False)
```

profile of v0, /device:TPU:0, one launch (start us, length us, event | category | flops | bytes accessed | tf_op | source)
XLA Modules:
  0.0 446.3 jit_solution(9777166148011291204)
XLA Ops:
  0.7 0.8 fusion.251
  1.4 4.9 %collective-permute-start = (f32[3,1,2,256]{3,2,1,0:T(2,128)S(1)}, f32[3,1,2,256]{3,2,1,0:T(2,128)S(1)}, u32[]{:S(2)}, u32[]{:S(2)}) collective-permute-start(f32[3,1,2,256]{3,2,1,0:T(2,128)S(1)} %get-tuple-element.267), channel_id=1, source_target_pairs={{0,8},{8,16},{16,24},{1,9},{9,17},{17,25},{2,10},{10,18},{18,26},{... | collective-permute-start | bytes 18440 | tf_op jit(solution)/shard_map/ppermute | solution.py:22
  6.3 1.3 collective-permute-start.1
  8.3 2.3 reduce-window.6
  14.0 5.0 %scatter_custom_fusion.1 = s32[2048]{0:T(1024)} fusion(s32[1024]{0:T(1024)S(1)} %broadcast_select_fusion.1, s32[1024]{0:T(1024)} %bitcast.117, s32[]{:T(128)} %constant.19.clone.1), kind=kCustom, calls=%fused_computation.834 | custom fusion | bytes 8704
  19.0 4.9 %all-to-all-start.1 = ((s32[1,8,256]{2,0,1:T(1,128)}), s32[1,8,256]{2,0,1:T(1,128)S(1)}, u32[]{:S(2)}, u32[]{:S(2)}) async-start(s32[1,8,256]{2,0,1:T(1,128)} %bitcast.18), calls=%async_computation.1 | async-start | bytes 16384 | tf_op jit(solution)/shard_map/all_to_all | solution.py:202
  25.4 2.4 collective-permute-start.2
  27.8 1.3 collective-permute-start.3
  30.8 1.3 collective-permute-done.3
  32.9 3.3 scatter_custom_fusion
  36.2 0.9 copy.26
  37.2 5.7 %all-to-all-start = ((f32[6,8,256]{2,0,1:T(8,128)}), f32[6,8,256]{2,0,1:T(8,128)S(1)}, u32[]{:S(2)}, u32[]{:S(2)}) async-start(f32[6,8,256]{2,0,1:T(8,128)} %copy.26), calls=%async_computation | async-start | bytes 131072 | tf_op jit(solution)/shard_map/all_to_all | solution.py:201
  43.1 5.8 %all-to-all-done = f32[6,8,256]{2,0,1:T(8,128)S(1)} async-done(((f32[6,8,256]{2,0,1:T(8,128)}), f32[6,8,256]{2,0,1:T(8,128)S(1)}, u32[]{:S(2)}, u32[]{:S(2)}) %all-to-all-start) | async-done | bytes 49184 | tf_op jit(solution)/shard_map/all_to_all | solution.py:201
  48.8 2.7 fusion.206
  51.6 6.6 %subtract_select_fusion.3 = f32[2048,512]{1,0:T(8,128)} fusion(pred[2048]{0:T(1024)(128)(4,1)S(1)} %gt.63, f32[2048,512]{1,0:T(8,128)} %fusion.206, bf16[1,512,512]{2,1,0:T(8,128)(2,1)S(1)} %copy-done, bf16[1,512,512]{2,1,0:T(8,128)(2,1)S(1)} %copy-done.6), kind=kOutput, calls=%fused_computation.13 | convolution fusion | flops 2152726528 | bytes 9439232 | tf_op jit(solution)/shard_map/dot_general | solution.py:112
  58.1 9.7 %subtract_select_fusion.2 = f32[2048,512]{1,0:T(8,128)} fusion(f32[2048,512]{1,0:T(8,128)} %subtract_select_fusion.3, pred[2048]{0:T(1024)(128)(4,1)S(1)} %gt.60, f32[2048,512]{1,0:T(8,128)} %fusion.206, bf16[1,512,512]{2,1,0:T(8,128)(2,1)S(1)} %copy-done, bf16[1,512,512]{2,1,0:T(8,128)(2,1)S(1)} %copy-done.6), kind=kOutput, calls=%fused_computation.5 | convolution fusion | flops 2155872256 | bytes 13633536 | tf_op jit(solution)/shard_map/dot_general | solution.py:112
  67.8 10.1 %subtract_select_fusion.1 = f32[2048,512]{1,0:T(8,128)} fusion(f32[2048,512]{1,0:T(8,128)} %subtract_select_fusion.2, pred[2048]{0:T(1024)(128)(4,1)S(1)} %gt.57, f32[2048,512]{1,0:T(8,128)} %fusion.206, bf16[1,512,512]{2,1,0:T(8,128)(2,1)S(1)} %copy-done, bf16[1,512,512]{2,1,0:T(8,128)(2,1)S(1)} %copy-done.6), kind=kOutput, calls=%fused_computation.4 | convolution fusion | flops 2155872256 | bytes 13633536 | tf_op jit(solution)/shard_map/dot_general | solution.py:112
  77.9 9.7 %subtract_select_fusion = f32[2048,512]{1,0:T(8,128)} fusion(f32[2048,512]{1,0:T(8,128)} %subtract_select_fusion.1, pred[2048]{0:T(1024)(128)(4,1)S(1)} %gt.54, f32[2048,512]{1,0:T(8,128)} %fusion.206, bf16[1,512,512]{2,1,0:T(8,128)(2,1)S(1)} %copy-done, bf16[1,512,512]{2,1,0:T(8,128)(2,1)S(1)} %copy-done.6), kind=kOutput, calls=%fused_computation.3 | convolution fusion | flops 2155872256 | bytes 13633536 | tf_op jit(solution)/shard_map/dot_general | solution.py:112
  87.8 3.0 fusion.7
  91.3 4.2 fusion.4
  95.7 0.9 copy.27
  96.6 3.6 all-to-all-start.2
  100.3 12.3 %all-to-all-done.2 = f32[42,8,256]{2,0,1:T(8,128)S(1)} async-done(((f32[42,8,256]{2,0,1:T(8,128)}), f32[42,8,256]{2,0,1:T(8,128)S(1)}, u32[]{:S(2)}, u32[]{:S(2)}) %all-to-all-start.2) | async-done | bytes 344096 | tf_op jit(solution)/shard_map/all_to_all | solution.py:215
  113.0 2.8 gather_fusion
  116.1 4.5 %collective-permute-start.4 = (f32[42,1,2,256]{3,2,1,0:T(2,128)S(1)}, f32[42,1,2,256]{3,2,1,0:T(2,128)S(1)}, u32[]{:S(2)}, u32[]{:S(2)}) collective-permute-start(f32[42,1,2,256]{3,2,1,0:T(2,128)S(1)} %slice.1305), channel_id=1, source_target_pairs={{0,8},{8,16},{16,24},{1,9},{9,17},{17,25},{2,10},{10,18},{18,26},{... | collective-permute-start | bytes 258056 | tf_op jit(solution)/shard_map/ppermute | solution.py:33
  120.7 2.1 collective-permute-done.4
  122.9 1.5 collective-permute-start.5
  126.1 4.3 collective-permute-start.6
  130.4 1.3 collective-permute-start.7
  131.7 5.5 %collective-permute-done.7 = f32[3,1,2,256]{3,2,1,0:T(2,128)S(1)} collective-permute-done((f32[3,1,2,256]{3,2,1,0:T(2,128)S(1)}, f32[3,1,2,256]{3,2,1,0:T(2,128)S(1)}, u32[]{:S(2)}, u32[]{:S(2)}) %collective-permute-start.7) | collective-permute-done | bytes 6176 | tf_op jit(solution)/shard_map/ppermute | solution.py:25
  137.2 2.0 collective-permute-start.8
  139.3 1.3 collective-permute-start.9
  140.8 4.6 %collective-permute-done.9 = f32[3,4,1,256]{3,2,1,0:T(1,128)S(1)} collective-permute-done((f32[3,4,1,256]{3,2,1,0:T(1,128)S(1)}, f32[3,4,1,256]{3,2,1,0:T(1,128)S(1)}, u32[]{:S(2)}, u32[]{:S(2)}) %collective-permute-start.9) | collective-permute-done | bytes 12320 | tf_op jit(solution)/shard_map/ppermute | solution.py:25
  147.5 42.8 %all-reduce.59 = (f32[]{:T(128)}, f32[]{:T(128)}) all-reduce(f32[]{:T(128)} %get-tuple-element.11, f32[]{:T(128)} %get-tuple-element.10), channel_id=1, replica_groups=mesh['macro'=4,'micro'=8] {'macro','micro'}, use_global_device_ids=true, to_apply=%region_6.7 | all-reduce | flops 2 | bytes 16 | tf_op jit(solution)/shard_map/psum | solution.py:168
  191.6 4.2 collective-permute-start.10
  195.8 1.3 collective-permute-start.11
  197.1 4.2 collective-permute-done.11
  201.4 1.3 collective-permute-start.12
  202.7 1.3 collective-permute-start.13
  204.0 2.5 collective-permute-done.13
  207.9 0.8 multiply_reduce_fusion.11
  208.7 42.4 %all-reduce.58 = (f32[]{:T(128)}, f32[]{:T(128)}) all-reduce(f32[]{:T(128)} %get-tuple-element.9, f32[]{:T(128)} %get-tuple-element.8), channel_id=1, replica_groups=mesh['macro'=4,'micro'=8] {'macro','micro'}, use_global_device_ids=true, to_apply=%region_11.12 | all-reduce | flops 2 | bytes 16 | tf_op jit(solution)/shard_map/psum | solution.py:168
  255.5 4.2 collective-permute-start.14
  259.7 1.3 collective-permute-start.15
  261.0 4.2 collective-permute-done.15
  265.2 1.3 collective-permute-start.16
  266.5 1.3 collective-permute-start.17
  267.9 2.5 collective-permute-done.17
  272.5 42.5 %all-reduce.57 = (f32[]{:T(128)}, f32[]{:T(128)}) all-reduce(f32[]{:T(128)} %get-tuple-element.7, f32[]{:T(128)} %get-tuple-element.6), channel_id=1, replica_groups=mesh['macro'=4,'micro'=8] {'macro','micro'}, use_global_device_ids=true, to_apply=%region_16.17 | all-reduce | flops 2 | bytes 16 | tf_op jit(solution)/shard_map/psum | solution.py:168
  318.8 4.2 collective-permute-start.18
  323.0 1.3 collective-permute-start.19
  324.3 4.2 collective-permute-done.19
  328.5 1.3 collective-permute-start.20
  329.8 1.3 collective-permute-start.21
  331.2 2.5 collective-permute-done.21
  335.1 0.8 multiply_reduce_fusion.7
  335.9 42.4 %all-reduce.56 = (f32[]{:T(128)}, f32[]{:T(128)}) all-reduce(f32[]{:T(128)} %get-tuple-element.5, f32[]{:T(128)} %get-tuple-element.4), channel_id=1, replica_groups=mesh['macro'=4,'micro'=8] {'macro','micro'}, use_global_device_ids=true, to_apply=%region_21.22 | all-reduce | flops 2 | bytes 16 | tf_op jit(solution)/shard_map/psum | solution.py:168
  382.2 4.2 collective-permute-start.22
  386.4 1.3 collective-permute-start.23
  387.8 4.2 collective-permute-done.23
  392.0 1.3 collective-permute-start.24
  393.3 1.3 collective-permute-start.25
  394.6 2.5 collective-permute-done.25
  399.3 42.4 %all-reduce.55 = (f32[]{:T(128)}, f32[]{:T(128)}) all-reduce(f32[]{:T(128)} %get-tuple-element.3, f32[]{:T(128)} %get-tuple-element.2), channel_id=1, replica_groups=mesh['macro'=4,'micro'=8] {'macro','micro'}, use_global_device_ids=true, to_apply=%region_26.27 | all-reduce | flops 2 | bytes 16 | tf_op jit(solution)/shard_map/psum | solution.py:168
  (256 shorter events, 19.9 us)
Async XLA Ops:
  0.6 50.9 %copy-start = (bf16[1,512,512]{2,1,0:T(8,128)(2,1)S(1)}, bf16[1,512,512]{2,1,0:T(8,128)(2,1)}, u32[]{:S(2)}) copy-start(bf16[1,512,512]{2,1,0:T(8,128)(2,1)} %param.15) | copy-start | bytes 1572868
  0.6 48.2 %copy-start.5 = (bf16[1,6,512]{2,1,0:T(8,128)(2,1)S(1)}, bf16[1,6,512]{2,1,0:T(8,128)(2,1)}, u32[]{:S(2)}) copy-start(bf16[1,6,512]{2,1,0:T(8,128)(2,1)} %param.16) | copy-start | bytes 18436
  1.4 23.2 %collective-permute-start = (f32[3,1,2,256]{3,2,1,0:T(2,128)S(1)}, f32[3,1,2,256]{3,2,1,0:T(2,128)S(1)}, u32[]{:S(2)}, u32[]{:S(2)}) collective-permute-start(f32[3,1,2,256]{3,2,1,0:T(2,128)S(1)} %get-tuple-element.267), channel_id=1, source_target_pairs={{0,8},{8,16},{16,24},{1,9},{9,17},{17,25},{2,10},{10,18},{18,26},{... | collective-permute-start | bytes 18440 | tf_op jit(solution)/shard_map/ppermute | solution.py:22
  6.3 19.1 %collective-permute-start.1 = (f32[3,1,2,256]{3,2,1,0:T(2,128)S(1)}, f32[3,1,2,256]{3,2,1,0:T(2,128)S(1)}, u32[]{:S(2)}, u32[]{:S(2)}) collective-permute-start(f32[3,1,2,256]{3,2,1,0:T(2,128)S(1)} %get-tuple-element.266), channel_id=1, source_target_pairs={{8,0},{16,8},{24,16},{9,1},{17,9},{25,17},{10,2},{18,10},{26,18},{... | collective-permute-start | bytes 18440 | tf_op jit(solution)/shard_map/ppermute | solution.py:25
  19.0 18.2 %all-to-all-start.1 = ((s32[1,8,256]{2,0,1:T(1,128)}), s32[1,8,256]{2,0,1:T(1,128)S(1)}, u32[]{:S(2)}, u32[]{:S(2)}) async-start(s32[1,8,256]{2,0,1:T(1,128)} %bitcast.18), calls=%async_computation.1 | async-start | bytes 16384 | tf_op jit(solution)/shard_map/all_to_all | solution.py:202
  25.4 5.4 %collective-permute-start.2 = (f32[3,4,1,256]{3,2,1,0:T(1,128)S(1)}, f32[3,4,1,256]{3,2,1,0:T(1,128)S(1)}, u32[]{:S(2)}, u32[]{:S(2)}) collective-permute-start(f32[3,4,1,256]{3,2,1,0:T(1,128)S(1)} %get-tuple-element.226), channel_id=1, source_target_pairs={{0,1},{1,2},{2,3},{3,4},{4,5},{5,6},{6,7},{8,9},{9,10},{10,11},{11... | collective-permute-start | bytes 36872 | tf_op jit(solution)/shard_map/ppermute | solution.py:22
  27.8 4.2 collective-permute-start.3
  30.6 21.0 %copy-start.6 = (bf16[1,512,512]{2,1,0:T(8,128)(2,1)S(1)}, bf16[1,512,512]{2,1,0:T(8,128)(2,1)}, u32[]{:S(2)}) copy-start(bf16[1,512,512]{2,1,0:T(8,128)(2,1)} %param.14) | copy-start | bytes 1572868
  37.2 11.6 %all-to-all-start = ((f32[6,8,256]{2,0,1:T(8,128)}), f32[6,8,256]{2,0,1:T(8,128)S(1)}, u32[]{:S(2)}, u32[]{:S(2)}) async-start(f32[6,8,256]{2,0,1:T(8,128)} %copy.26), calls=%async_computation | async-start | bytes 131072 | tf_op jit(solution)/shard_map/all_to_all | solution.py:201
  77.9 9.9 %copy-start.3 = (bf16[1,512,6]{1,2,0:T(8,128)(2,1)S(1)}, bf16[1,512,6]{1,2,0:T(8,128)(2,1)}, u32[]{:S(2)}) copy-start(bf16[1,512,6]{1,2,0:T(8,128)(2,1)} %param.17) | copy-start | bytes 18436
  87.8 3.5 copy-start.1
  91.3 8.9 %copy-start.2 = (s32[1,1,1024,1]{2,3,1,0:T(1,128)S(1)}, s32[1,1,1024,1]{2,3,1,0:T(1,128)}, u32[]{:S(2)}) copy-start(s32[1,1,1024,1]{2,3,1,0:T(1,128)} %param.12) | copy-start | bytes 12292
  96.6 29.3 %copy-start.4 = (f32[3,2,2,256]{3,2,1,0:T(2,128)S(1)}, f32[3,2,2,256]{3,2,1,0:T(2,128)}, u32[]{:S(2)}) copy-start(f32[3,2,2,256]{3,2,1,0:T(2,128)} %param.11) | copy-start | bytes 36868
  96.6 16.0 %all-to-all-start.2 = ((f32[42,8,256]{2,0,1:T(8,128)}), f32[42,8,256]{2,0,1:T(8,128)S(1)}, u32[]{:S(2)}, u32[]{:S(2)}) async-start(f32[42,8,256]{2,0,1:T(8,128)} %copy.27), calls=%async_computation.2 | async-start | bytes 786432 | tf_op jit(solution)/shard_map/all_to_all | solution.py:215
  116.1 6.6 %collective-permute-start.4 = (f32[42,1,2,256]{3,2,1,0:T(2,128)S(1)}, f32[42,1,2,256]{3,2,1,0:T(2,128)S(1)}, u32[]{:S(2)}, u32[]{:S(2)}) collective-permute-start(f32[42,1,2,256]{3,2,1,0:T(2,128)S(1)} %slice.1305), channel_id=1, source_target_pairs={{0,8},{8,16},{16,24},{1,9},{9,17},{17,25},{2,10},{10,18},{18,26},{... | collective-permute-start | bytes 258056 | tf_op jit(solution)/shard_map/ppermute | solution.py:33
  122.9 2.3 collective-permute-start.5
  126.1 5.6 %collective-permute-start.6 = (f32[3,1,2,256]{3,2,1,0:T(2,128)S(1)}, f32[3,1,2,256]{3,2,1,0:T(2,128)S(1)}, u32[]{:S(2)}, u32[]{:S(2)}) collective-permute-start(f32[3,1,2,256]{3,2,1,0:T(2,128)S(1)} %get-tuple-element.259), channel_id=1, source_target_pairs={{0,8},{8,16},{16,24},{1,9},{9,17},{17,25},{2,10},{10,18},{18,26},{... | collective-permute-start | bytes 18440 | tf_op jit(solution)/shard_map/ppermute | solution.py:22
  130.4 6.8 %collective-permute-start.7 = (f32[3,1,2,256]{3,2,1,0:T(2,128)S(1)}, f32[3,1,2,256]{3,2,1,0:T(2,128)S(1)}, u32[]{:S(2)}, u32[]{:S(2)}) collective-permute-start(f32[3,1,2,256]{3,2,1,0:T(2,128)S(1)} %get-tuple-element.260), channel_id=1, source_target_pairs={{8,0},{16,8},{24,16},{9,1},{17,9},{25,17},{10,2},{18,10},{26,18},{... | collective-permute-start | bytes 18440 | tf_op jit(solution)/shard_map/ppermute | solution.py:25
  137.2 3.5 collective-permute-start.8
  139.3 6.1 %collective-permute-start.9 = (f32[3,4,1,256]{3,2,1,0:T(1,128)S(1)}, f32[3,4,1,256]{3,2,1,0:T(1,128)S(1)}, u32[]{:S(2)}, u32[]{:S(2)}) collective-permute-start(f32[3,4,1,256]{3,2,1,0:T(1,128)S(1)} %get-tuple-element.224), channel_id=1, source_target_pairs={{1,0},{2,1},{3,2},{4,3},{5,4},{6,5},{7,6},{9,8},{10,9},{11,10},{12... | collective-permute-start | bytes 36872 | tf_op jit(solution)/shard_map/ppermute | solution.py:25
  191.6 5.5 %collective-permute-start.10 = (f32[3,1,2,256]{3,2,1,0:T(2,128)S(1)}, f32[3,1,2,256]{3,2,1,0:T(2,128)S(1)}, u32[]{:S(2)}, u32[]{:S(2)}) collective-permute-start(f32[3,1,2,256]{3,2,1,0:T(2,128)S(1)} %get-tuple-element.257), channel_id=1, source_target_pairs={{0,8},{8,16},{16,24},{1,9},{9,17},{17,25},{2,10},{10,18},{18,26},{... | collective-permute-start | bytes 18440 | tf_op jit(solution)/shard_map/ppermute | solution.py:22
  195.8 5.5 %collective-permute-start.11 = (f32[3,1,2,256]{3,2,1,0:T(2,128)S(1)}, f32[3,1,2,256]{3,2,1,0:T(2,128)S(1)}, u32[]{:S(2)}, u32[]{:S(2)}) collective-permute-start(f32[3,1,2,256]{3,2,1,0:T(2,128)S(1)} %get-tuple-element.258), channel_id=1, source_target_pairs={{8,0},{16,8},{24,16},{9,1},{17,9},{25,17},{10,2},{18,10},{26,18},{... | collective-permute-start | bytes 18440 | tf_op jit(solution)/shard_map/ppermute | solution.py:25
  201.4 2.6 collective-permute-start.12
  202.7 3.8 collective-permute-start.13
  255.5 5.5 %collective-permute-start.14 = (f32[3,1,2,256]{3,2,1,0:T(2,128)S(1)}, f32[3,1,2,256]{3,2,1,0:T(2,128)S(1)}, u32[]{:S(2)}, u32[]{:S(2)}) collective-permute-start(f32[3,1,2,256]{3,2,1,0:T(2,128)S(1)} %get-tuple-element.255), channel_id=1, source_target_pairs={{0,8},{8,16},{16,24},{1,9},{9,17},{17,25},{2,10},{10,18},{18,26},{... | collective-permute-start | bytes 18440 | tf_op jit(solution)/shard_map/ppermute | solution.py:22
  259.7 5.5 %collective-permute-start.15 = (f32[3,1,2,256]{3,2,1,0:T(2,128)S(1)}, f32[3,1,2,256]{3,2,1,0:T(2,128)S(1)}, u32[]{:S(2)}, u32[]{:S(2)}) collective-permute-start(f32[3,1,2,256]{3,2,1,0:T(2,128)S(1)} %get-tuple-element.256), channel_id=1, source_target_pairs={{8,0},{16,8},{24,16},{9,1},{17,9},{25,17},{10,2},{18,10},{26,18},{... | collective-permute-start | bytes 18440 | tf_op jit(solution)/shard_map/ppermute | solution.py:25
  265.2 2.6 collective-permute-start.16
  266.5 3.8 collective-permute-start.17
  318.8 5.5 %collective-permute-start.18 = (f32[3,1,2,256]{3,2,1,0:T(2,128)S(1)}, f32[3,1,2,256]{3,2,1,0:T(2,128)S(1)}, u32[]{:S(2)}, u32[]{:S(2)}) collective-permute-start(f32[3,1,2,256]{3,2,1,0:T(2,128)S(1)} %get-tuple-element.253), channel_id=1, source_target_pairs={{0,8},{8,16},{16,24},{1,9},{9,17},{17,25},{2,10},{10,18},{18,26},{... | collective-permute-start | bytes 18440 | tf_op jit(solution)/shard_map/ppermute | solution.py:22
  323.0 5.5 %collective-permute-start.19 = (f32[3,1,2,256]{3,2,1,0:T(2,128)S(1)}, f32[3,1,2,256]{3,2,1,0:T(2,128)S(1)}, u32[]{:S(2)}, u32[]{:S(2)}) collective-permute-start(f32[3,1,2,256]{3,2,1,0:T(2,128)S(1)} %get-tuple-element.254), channel_id=1, source_target_pairs={{8,0},{16,8},{24,16},{9,1},{17,9},{25,17},{10,2},{18,10},{26,18},{... | collective-permute-start | bytes 18440 | tf_op jit(solution)/shard_map/ppermute | solution.py:25
  328.5 2.6 collective-permute-start.20
  329.8 3.8 collective-permute-start.21
  382.2 5.5 %collective-permute-start.22 = (f32[3,1,2,256]{3,2,1,0:T(2,128)S(1)}, f32[3,1,2,256]{3,2,1,0:T(2,128)S(1)}, u32[]{:S(2)}, u32[]{:S(2)}) collective-permute-start(f32[3,1,2,256]{3,2,1,0:T(2,128)S(1)} %get-tuple-element.251), channel_id=1, source_target_pairs={{0,8},{8,16},{16,24},{1,9},{9,17},{17,25},{2,10},{10,18},{18,26},{... | collective-permute-start | bytes 18440 | tf_op jit(solution)/shard_map/ppermute | solution.py:22
  386.4 5.5 %collective-permute-start.23 = (f32[3,1,2,256]{3,2,1,0:T(2,128)S(1)}, f32[3,1,2,256]{3,2,1,0:T(2,128)S(1)}, u32[]{:S(2)}, u32[]{:S(2)}) collective-permute-start(f32[3,1,2,256]{3,2,1,0:T(2,128)S(1)} %get-tuple-element.252), channel_id=1, source_target_pairs={{8,0},{16,8},{24,16},{9,1},{17,9},{25,17},{10,2},{18,10},{26,18},{... | collective-permute-start | bytes 18440 | tf_op jit(solution)/shard_map/ppermute | solution.py:25
  392.0 2.6 collective-permute-start.24
  393.3 3.8 collective-permute-start.25
where the time goes:
time: 449 us; the launch traced here: 446 us
  blocking collectives  212 us (47%)
  starting transfers between devices  71.2 us (16%)
  waiting for transfers between devices  59.1 us (13%)
  matrix products  46 us (10%)
  between operations  20.8 us (5%)
  other arithmetic  19.8 us (4%)
  local copies, waits for them, and re-layouts  17 us (4%)
    psum x5, blocking collectives, two_products(): lax.psum((jnp.sum(residual * residual), jnp.sum(residual * image)), ('mac...  212 us
    ppermute x12, waiting for transfers between devices, with_halo(): lax.ppermute(lax.slice_in_dim(block, 0, width, axis=dim), axis, backward)  38.2 us
    dot_general x4, matrix products, micro_solve(): jnp.dot(misfit.astype(jnp.bfloat16), precond, preferred_element_type=jnp....  36.1 us
    ppermute x12, starting transfers between devices, with_halo(): lax.ppermute(lax.slice_in_dim(block, block.shape[dim] - width, None, axis...  35.5 us
    ppermute x12, starting transfers between devices, with_halo(): lax.ppermute(lax.slice_in_dim(block, 0, width, axis=dim), axis, backward)  15.5 us
    all_to_all x1, waiting for transfers between devices, shards(): lax.all_to_all(rows, 'micro', split_axis=1, concat_axis=1, tiled=True)  12.3 us
  transfers between devices with their start and end apart: 29, of which 15 were waited for; matrix products, arithmetic and copies ran while one was open for 4% of the time, Pallas kernels for 0%

commit v1 on v0

--- a/solution.py
+++ b/solution.py
@@ -165,7 +165,9 @@
 
 
 def two_products(residual, image):
-    return lax.psum((jnp.sum(residual * residual), jnp.sum(residual * image)), ("macro", "micro"))
+    return lax.psum(
+        lax.psum((jnp.sum(residual * residual), jnp.sum(residual * image)), "micro"), "macro"
+    )
 
 
 def shards(

time: 449 us -> 360 us (0.80)
  blocking collectives: 212 us -> 132 us
  starting transfers between devices: 71.2 us -> 61.1 us
    psum x5 -> x10, blocking collectives: 212 us -> 132 us  [the longest x5 77.4 us: two_products(): lax.psum((jnp.sum(residual * residual), jnp.sum(residual * image)), 'micro')]
    ppermute x12, starting transfers between devices: 35.5 us -> 25.4 us  [with_halo(): lax.ppermute(lax.slice_in_dim(block, block.shape[dim] - width, None, axis...]
  transfers between devices with their start and end apart: 29 -> 29, of which waited for: 15 -> 15; matrix products, arithmetic and copies ran while one was open for 4% -> 5% of each run, Pallas kernels for 0% -> 0%
where the time goes in v1:
time: 360 us; the launch traced here: 358 us
  blocking collectives  132 us (37%)
  starting transfers between devices  61.1 us (17%)
  waiting for transfers between devices  60.8 us (17%)
  matrix products  45.9 us (13%)
  between operations  21.1 us (6%)
  other arithmetic  19.8 us (6%)
  local copies, waits for them, and re-layouts  17 us (5%)
    psum x5, blocking collectives, two_products(): lax.psum((jnp.sum(residual * residual), jnp.sum(residual * image)), 'micro')  77.4 us
    psum x5, blocking collectives, two_products(): lax.psum(lax.psum((jnp.sum(residual * residual), jnp.sum(residual * image...  55.1 us
    ppermute x12, waiting for transfers between devices, with_halo(): lax.ppermute(lax.slice_in_dim(block, 0, width, axis=dim), axis, backward)  39.8 us
    dot_general x4, matrix products, micro_solve(): jnp.dot(misfit.astype(jnp.bfloat16), precond, preferred_element_type=jnp....  36 us
    ppermute x12, starting transfers between devices, with_halo(): lax.ppermute(lax.slice_in_dim(block, block.shape[dim] - width, None, axis...  25.4 us
    ppermute x12, starting transfers between devices, with_halo(): lax.ppermute(lax.slice_in_dim(block, 0, width, axis=dim), axis, backward)  15.5 us
    all_to_all x1, waiting for transfers between devices, shards(): lax.all_to_all(rows, 'micro', split_axis=1, concat_axis=1, tiled=True)  12.3 us
  transfers between devices with their start and end apart: 29, of which 15 were waited for; matrix products, arithmetic and copies ran while one was open for 5% of the time, Pallas kernels for 0%

profile of v1, /device:TPU:0, one launch (start us, length us, event | category | flops | bytes accessed | tf_op | source)
XLA Modules:
  0.0 358.2 jit_solution(8629706075465855807)
XLA Ops:
  1.4 4.9 %collective-permute-start = (f32[3,1,2,256]{3,2,1,0:T(2,128)S(1)}, f32[3,1,2,256]{3,2,1,0:T(2,128)S(1)}, u32[]{:S(2)}, u32[]{:S(2)}) collective-permute-start(f32[3,1,2,256]{3,2,1,0:T(2,128)S(1)} %get-tuple-element.277), channel_id=1, source_target_pairs={{0,8},{8,16},{16,24},{1,9},{9,17},{17,25},{2,10},{10,18},{18,26},{... | collective-permute-start | bytes 18440 | tf_op jit(solution)/shard_map/ppermute | solution.py:22
  6.3 1.3 collective-permute-start.1
  8.3 2.3 reduce-window.6
  14.0 5.0 %scatter_custom_fusion.1 = s32[2048]{0:T(1024)} fusion(s32[1024]{0:T(1024)S(1)} %broadcast_select_fusion.1, s32[1024]{0:T(1024)} %bitcast.117, s32[]{:T(128)} %constant.19.clone.1), kind=kCustom, calls=%fused_computation.834 | custom fusion | bytes 8704
  19.0 4.9 %all-to-all-start.1 = ((s32[1,8,256]{2,0,1:T(1,128)}), s32[1,8,256]{2,0,1:T(1,128)S(1)}, u32[]{:S(2)}, u32[]{:S(2)}) async-start(s32[1,8,256]{2,0,1:T(1,128)} %bitcast.18), calls=%async_computation.1 | async-start | bytes 16384 | tf_op jit(solution)/shard_map/all_to_all | solution.py:204
  25.4 2.4 collective-permute-start.2
  27.8 1.3 collective-permute-start.3
  30.8 1.3 collective-permute-done.3
  32.9 3.3 scatter_custom_fusion
  37.2 5.7 %all-to-all-start = ((f32[6,8,256]{2,0,1:T(8,128)}), f32[6,8,256]{2,0,1:T(8,128)S(1)}, u32[]{:S(2)}, u32[]{:S(2)}) async-start(f32[6,8,256]{2,0,1:T(8,128)} %copy.26), calls=%async_computation | async-start | bytes 131072 | tf_op jit(solution)/shard_map/all_to_all | solution.py:203
  43.1 5.8 %all-to-all-done = f32[6,8,256]{2,0,1:T(8,128)S(1)} async-done(((f32[6,8,256]{2,0,1:T(8,128)}), f32[6,8,256]{2,0,1:T(8,128)S(1)}, u32[]{:S(2)}, u32[]{:S(2)}) %all-to-all-start) | async-done | bytes 49184 | tf_op jit(solution)/shard_map/all_to_all | solution.py:203
  48.8 2.7 fusion.206
  51.5 6.6 %subtract_select_fusion.3 = f32[2048,512]{1,0:T(8,128)} fusion(pred[2048]{0:T(1024)(128)(4,1)S(1)} %gt.63, f32[2048,512]{1,0:T(8,128)} %fusion.206, bf16[1,512,512]{2,1,0:T(8,128)(2,1)S(1)} %copy-done, bf16[1,512,512]{2,1,0:T(8,128)(2,1)S(1)} %copy-done.6), kind=kOutput, calls=%fused_computation.13 | convolution fusion | flops 2152726528 | bytes 9439232 | tf_op jit(solution)/shard_map/dot_general | solution.py:112
  58.1 9.7 %subtract_select_fusion.2 = f32[2048,512]{1,0:T(8,128)} fusion(f32[2048,512]{1,0:T(8,128)} %subtract_select_fusion.3, pred[2048]{0:T(1024)(128)(4,1)S(1)} %gt.60, f32[2048,512]{1,0:T(8,128)} %fusion.206, bf16[1,512,512]{2,1,0:T(8,128)(2,1)S(1)} %copy-done, bf16[1,512,512]{2,1,0:T(8,128)(2,1)S(1)} %copy-done.6), kind=kOutput, calls=%fused_computation.5 | convolution fusion | flops 2155872256 | bytes 13633536 | tf_op jit(solution)/shard_map/dot_general | solution.py:112
  67.8 10.0 %subtract_select_fusion.1 = f32[2048,512]{1,0:T(8,128)} fusion(f32[2048,512]{1,0:T(8,128)} %subtract_select_fusion.2, pred[2048]{0:T(1024)(128)(4,1)S(1)} %gt.57, f32[2048,512]{1,0:T(8,128)} %fusion.206, bf16[1,512,512]{2,1,0:T(8,128)(2,1)S(1)} %copy-done, bf16[1,512,512]{2,1,0:T(8,128)(2,1)S(1)} %copy-done.6), kind=kOutput, calls=%fused_computation.4 | convolution fusion | flops 2155872256 | bytes 13633536 | tf_op jit(solution)/shard_map/dot_general | solution.py:112
  77.8 9.7 %subtract_select_fusion = f32[2048,512]{1,0:T(8,128)} fusion(f32[2048,512]{1,0:T(8,128)} %subtract_select_fusion.1, pred[2048]{0:T(1024)(128)(4,1)S(1)} %gt.54, f32[2048,512]{1,0:T(8,128)} %fusion.206, bf16[1,512,512]{2,1,0:T(8,128)(2,1)S(1)} %copy-done, bf16[1,512,512]{2,1,0:T(8,128)(2,1)S(1)} %copy-done.6), kind=kOutput, calls=%fused_computation.3 | convolution fusion | flops 2155872256 | bytes 13633536 | tf_op jit(solution)/shard_map/dot_general | solution.py:112
  87.7 3.0 fusion.7
  91.1 4.2 %fusion.4 = f32[36,2048]{1,0:T(8,128)S(1)} fusion(f32[512,36]{0,1:T(8,128)S(1)} %stack.124, f32[2048,512]{1,0:T(8,128)S(1)} %copy-done.1, f32[36]{0:T(128)S(1)} %stack.129), kind=kOutput, calls=%fused_computation.15 | convolution fusion | flops 455155712 | bytes 4563088 | tf_op jit(solution)/shard_map/dot_general | solution.py:136
  96.4 3.6 %all-to-all-start.2 = ((f32[42,8,256]{2,0,1:T(8,128)}), f32[42,8,256]{2,0,1:T(8,128)S(1)}, u32[]{:S(2)}, u32[]{:S(2)}) async-start(f32[42,8,256]{2,0,1:T(8,128)} %copy.27), calls=%async_computation.2 | async-start | bytes 786432 | tf_op jit(solution)/shard_map/all_to_all | solution.py:217
  100.2 12.3 %all-to-all-done.2 = f32[42,8,256]{2,0,1:T(8,128)S(1)} async-done(((f32[42,8,256]{2,0,1:T(8,128)}), f32[42,8,256]{2,0,1:T(8,128)S(1)}, u32[]{:S(2)}, u32[]{:S(2)}) %all-to-all-start.2) | async-done | bytes 344096 | tf_op jit(solution)/shard_map/all_to_all | solution.py:217
  112.8 2.8 gather_fusion
  116.0 4.5 %collective-permute-start.4 = (f32[42,1,2,256]{3,2,1,0:T(2,128)S(1)}, f32[42,1,2,256]{3,2,1,0:T(2,128)S(1)}, u32[]{:S(2)}, u32[]{:S(2)}) collective-permute-start(f32[42,1,2,256]{3,2,1,0:T(2,128)S(1)} %slice.1305), channel_id=1, source_target_pairs={{0,8},{8,16},{16,24},{1,9},{9,17},{17,25},{2,10},{10,18},{18,26},{... | collective-permute-start | bytes 258056 | tf_op jit(solution)/shard_map/ppermute | solution.py:33
  120.6 2.1 collective-permute-done.4
  122.8 1.5 collective-permute-start.5
  126.0 4.3 %collective-permute-start.6 = (f32[3,1,2,256]{3,2,1,0:T(2,128)S(1)}, f32[3,1,2,256]{3,2,1,0:T(2,128)S(1)}, u32[]{:S(2)}, u32[]{:S(2)}) collective-permute-start(f32[3,1,2,256]{3,2,1,0:T(2,128)S(1)} %get-tuple-element.269), channel_id=1, source_target_pairs={{0,8},{8,16},{16,24},{1,9},{9,17},{17,25},{2,10},{10,18},{18,26},{... | collective-permute-start | bytes 18440 | tf_op jit(solution)/shard_map/ppermute | solution.py:22
  130.3 1.3 collective-permute-start.7
  131.6 5.5 %collective-permute-done.7 = f32[3,1,2,256]{3,2,1,0:T(2,128)S(1)} collective-permute-done((f32[3,1,2,256]{3,2,1,0:T(2,128)S(1)}, f32[3,1,2,256]{3,2,1,0:T(2,128)S(1)}, u32[]{:S(2)}, u32[]{:S(2)}) %collective-permute-start.7) | collective-permute-done | bytes 6176 | tf_op jit(solution)/shard_map/ppermute | solution.py:25
  137.1 2.0 collective-permute-start.8
  139.2 1.3 collective-permute-start.9
  140.7 4.6 %collective-permute-done.9 = f32[3,4,1,256]{3,2,1,0:T(1,128)S(1)} collective-permute-done((f32[3,4,1,256]{3,2,1,0:T(1,128)S(1)}, f32[3,4,1,256]{3,2,1,0:T(1,128)S(1)}, u32[]{:S(2)}, u32[]{:S(2)}) %collective-permute-start.9) | collective-permute-done | bytes 12320 | tf_op jit(solution)/shard_map/ppermute | solution.py:25
  147.4 16.6 %all-reduce.59 = (f32[]{:T(128)}, f32[]{:T(128)}) all-reduce(f32[]{:T(128)} %get-tuple-element.11, f32[]{:T(128)} %get-tuple-element.10), channel_id=1, replica_groups=mesh['macro'=4,'micro'=8] {'micro'}, use_global_device_ids=true, to_apply=%region_6.7 | all-reduce | flops 2 | bytes 16 | tf_op jit(solution)/shard_map/psum | solution.py:169
  164.1 11.0 %all-reduce.64 = (f32[]{:T(128)}, f32[]{:T(128)}) all-reduce(f32[]{:T(128)} %get-tuple-element.24, f32[]{:T(128)} %get-tuple-element.25), channel_id=1, replica_groups=mesh['macro'=4,'micro'=8] {'macro'}, use_global_device_ids=true, to_apply=%region_7.8 | all-reduce | flops 2 | bytes 16 | tf_op jit(solution)/shard_map/psum | solution.py:168
  176.4 1.6 collective-permute-start.10
  178.1 1.3 collective-permute-start.11
  179.4 5.4 %collective-permute-done.11 = f32[3,1,2,256]{3,2,1,0:T(2,128)S(1)} collective-permute-done((f32[3,1,2,256]{3,2,1,0:T(2,128)S(1)}, f32[3,1,2,256]{3,2,1,0:T(2,128)S(1)}, u32[]{:S(2)}, u32[]{:S(2)}) %collective-permute-start.11) | collective-permute-done | bytes 6176 | tf_op jit(solution)/shard_map/ppermute | solution.py:25
  184.8 1.3 collective-permute-start.12
  186.1 1.3 collective-permute-start.13
  187.4 1.8 collective-permute-done.13
  191.4 15.2 %all-reduce.58 = (f32[]{:T(128)}, f32[]{:T(128)}) all-reduce(f32[]{:T(128)} %get-tuple-element.9, f32[]{:T(128)} %get-tuple-element.8), channel_id=1, replica_groups=mesh['macro'=4,'micro'=8] {'micro'}, use_global_device_ids=true, to_apply=%region_13.14 | all-reduce | flops 2 | bytes 16 | tf_op jit(solution)/shard_map/psum | solution.py:169
  206.6 11.1 %all-reduce.63 = (f32[]{:T(128)}, f32[]{:T(128)}) all-reduce(f32[]{:T(128)} %get-tuple-element.22, f32[]{:T(128)} %get-tuple-element.23), channel_id=1, replica_groups=mesh['macro'=4,'micro'=8] {'macro'}, use_global_device_ids=true, to_apply=%region_14.15 | all-reduce | flops 2 | bytes 16 | tf_op jit(solution)/shard_map/psum | solution.py:168
  222.1 1.6 collective-permute-start.14
  223.7 1.3 collective-permute-start.15
  225.0 5.4 %collective-permute-done.15 = f32[3,1,2,256]{3,2,1,0:T(2,128)S(1)} collective-permute-done((f32[3,1,2,256]{3,2,1,0:T(2,128)S(1)}, f32[3,1,2,256]{3,2,1,0:T(2,128)S(1)}, u32[]{:S(2)}, u32[]{:S(2)}) %collective-permute-start.15) | collective-permute-done | bytes 6176 | tf_op jit(solution)/shard_map/ppermute | solution.py:25
  230.4 1.3 collective-permute-start.16
  231.7 1.3 collective-permute-start.17
  233.1 1.8 collective-permute-done.17
  237.0 15.2 %all-reduce.57 = (f32[]{:T(128)}, f32[]{:T(128)}) all-reduce(f32[]{:T(128)} %get-tuple-element.7, f32[]{:T(128)} %get-tuple-element.6), channel_id=1, replica_groups=mesh['macro'=4,'micro'=8] {'micro'}, use_global_device_ids=true, to_apply=%region_20.21 | all-reduce | flops 2 | bytes 16 | tf_op jit(solution)/shard_map/psum | solution.py:169
  252.2 11.0 %all-reduce.62 = (f32[]{:T(128)}, f32[]{:T(128)}) all-reduce(f32[]{:T(128)} %get-tuple-element.20, f32[]{:T(128)} %get-tuple-element.21), channel_id=1, replica_groups=mesh['macro'=4,'micro'=8] {'macro'}, use_global_device_ids=true, to_apply=%region_21.22 | all-reduce | flops 2 | bytes 16 | tf_op jit(solution)/shard_map/psum | solution.py:168
  267.0 1.6 collective-permute-start.18
  268.6 1.3 collective-permute-start.19
  270.0 5.4 %collective-permute-done.19 = f32[3,1,2,256]{3,2,1,0:T(2,128)S(1)} collective-permute-done((f32[3,1,2,256]{3,2,1,0:T(2,128)S(1)}, f32[3,1,2,256]{3,2,1,0:T(2,128)S(1)}, u32[]{:S(2)}, u32[]{:S(2)}) %collective-permute-start.19) | collective-permute-done | bytes 6176 | tf_op jit(solution)/shard_map/ppermute | solution.py:25
  275.4 1.3 collective-permute-start.20
  276.7 1.3 collective-permute-start.21
  278.0 1.8 collective-permute-done.21
  282.0 15.2 %all-reduce.56 = (f32[]{:T(128)}, f32[]{:T(128)}) all-reduce(f32[]{:T(128)} %get-tuple-element.5, f32[]{:T(128)} %get-tuple-element.4), channel_id=1, replica_groups=mesh['macro'=4,'micro'=8] {'micro'}, use_global_device_ids=true, to_apply=%region_27.28 | all-reduce | flops 2 | bytes 16 | tf_op jit(solution)/shard_map/psum | solution.py:169
  297.2 11.1 %all-reduce.61 = (f32[]{:T(128)}, f32[]{:T(128)}) all-reduce(f32[]{:T(128)} %get-tuple-element.18, f32[]{:T(128)} %get-tuple-element.19), channel_id=1, replica_groups=mesh['macro'=4,'micro'=8] {'macro'}, use_global_device_ids=true, to_apply=%region_28.29 | all-reduce | flops 2 | bytes 16 | tf_op jit(solution)/shard_map/psum | solution.py:168
  312.4 1.6 collective-permute-start.22
  314.0 1.3 collective-permute-start.23
  315.4 5.4 %collective-permute-done.23 = f32[3,1,2,256]{3,2,1,0:T(2,128)S(1)} collective-permute-done((f32[3,1,2,256]{3,2,1,0:T(2,128)S(1)}, f32[3,1,2,256]{3,2,1,0:T(2,128)S(1)}, u32[]{:S(2)}, u32[]{:S(2)}) %collective-permute-start.23) | collective-permute-done | bytes 6176 | tf_op jit(solution)/shard_map/ppermute | solution.py:25
  320.8 1.3 collective-permute-start.24
  322.1 1.3 collective-permute-start.25
  323.4 1.8 collective-permute-done.25
  327.3 15.2 %all-reduce.55 = (f32[]{:T(128)}, f32[]{:T(128)}) all-reduce(f32[]{:T(128)} %get-tuple-element.3, f32[]{:T(128)} %get-tuple-element.2), channel_id=1, replica_groups=mesh['macro'=4,'micro'=8] {'micro'}, use_global_device_ids=true, to_apply=%region_34.35 | all-reduce | flops 2 | bytes 16 | tf_op jit(solution)/shard_map/psum | solution.py:169
  342.5 11.0 %all-reduce.60 = (f32[]{:T(128)}, f32[]{:T(128)}) all-reduce(f32[]{:T(128)} %get-tuple-element.16, f32[]{:T(128)} %get-tuple-element.17), channel_id=1, replica_groups=mesh['macro'=4,'micro'=8] {'macro'}, use_global_device_ids=true, to_apply=%region_35.36 | all-reduce | flops 2 | bytes 16 | tf_op jit(solution)/shard_map/psum | solution.py:168
  (261 shorter events, 24.2 us)
Async XLA Ops:
  0.6 50.9 %copy-start = (bf16[1,512,512]{2,1,0:T(8,128)(2,1)S(1)}, bf16[1,512,512]{2,1,0:T(8,128)(2,1)}, u32[]{:S(2)}) copy-start(bf16[1,512,512]{2,1,0:T(8,128)(2,1)} %param.15) | copy-start | bytes 1572868
  0.6 48.2 %copy-start.5 = (bf16[1,6,512]{2,1,0:T(8,128)(2,1)S(1)}, bf16[1,6,512]{2,1,0:T(8,128)(2,1)}, u32[]{:S(2)}) copy-start(bf16[1,6,512]{2,1,0:T(8,128)(2,1)} %param.16) | copy-start | bytes 18436
  1.4 23.2 %collective-permute-start = (f32[3,1,2,256]{3,2,1,0:T(2,128)S(1)}, f32[3,1,2,256]{3,2,1,0:T(2,128)S(1)}, u32[]{:S(2)}, u32[]{:S(2)}) collective-permute-start(f32[3,1,2,256]{3,2,1,0:T(2,128)S(1)} %get-tuple-element.277), channel_id=1, source_target_pairs={{0,8},{8,16},{16,24},{1,9},{9,17},{17,25},{2,10},{10,18},{18,26},{... | collective-permute-start | bytes 18440 | tf_op jit(solution)/shard_map/ppermute | solution.py:22
  6.3 19.1 %collective-permute-start.1 = (f32[3,1,2,256]{3,2,1,0:T(2,128)S(1)}, f32[3,1,2,256]{3,2,1,0:T(2,128)S(1)}, u32[]{:S(2)}, u32[]{:S(2)}) collective-permute-start(f32[3,1,2,256]{3,2,1,0:T(2,128)S(1)} %get-tuple-element.276), channel_id=1, source_target_pairs={{8,0},{16,8},{24,16},{9,1},{17,9},{25,17},{10,2},{18,10},{26,18},{... | collective-permute-start | bytes 18440 | tf_op jit(solution)/shard_map/ppermute | solution.py:25
  19.0 18.2 %all-to-all-start.1 = ((s32[1,8,256]{2,0,1:T(1,128)}), s32[1,8,256]{2,0,1:T(1,128)S(1)}, u32[]{:S(2)}, u32[]{:S(2)}) async-start(s32[1,8,256]{2,0,1:T(1,128)} %bitcast.18), calls=%async_computation.1 | async-start | bytes 16384 | tf_op jit(solution)/shard_map/all_to_all | solution.py:204
  25.4 5.4 %collective-permute-start.2 = (f32[3,4,1,256]{3,2,1,0:T(1,128)S(1)}, f32[3,4,1,256]{3,2,1,0:T(1,128)S(1)}, u32[]{:S(2)}, u32[]{:S(2)}) collective-permute-start(f32[3,4,1,256]{3,2,1,0:T(1,128)S(1)} %get-tuple-element.236), channel_id=1, source_target_pairs={{0,1},{1,2},{2,3},{3,4},{4,5},{5,6},{6,7},{8,9},{9,10},{10,11},{11... | collective-permute-start | bytes 36872 | tf_op jit(solution)/shard_map/ppermute | solution.py:22
  27.8 4.2 %collective-permute-start.3 = (f32[3,4,1,256]{3,2,1,0:T(1,128)S(1)}, f32[3,4,1,256]{3,2,1,0:T(1,128)S(1)}, u32[]{:S(2)}, u32[]{:S(2)}) collective-permute-start(f32[3,4,1,256]{3,2,1,0:T(1,128)S(1)} %get-tuple-element.237), channel_id=1, source_target_pairs={{1,0},{2,1},{3,2},{4,3},{5,4},{6,5},{7,6},{9,8},{10,9},{11,10},{12... | collective-permute-start | bytes 36872 | tf_op jit(solution)/shard_map/ppermute | solution.py:25
  30.6 20.9 %copy-start.6 = (bf16[1,512,512]{2,1,0:T(8,128)(2,1)S(1)}, bf16[1,512,512]{2,1,0:T(8,128)(2,1)}, u32[]{:S(2)}) copy-start(bf16[1,512,512]{2,1,0:T(8,128)(2,1)} %param.14) | copy-start | bytes 1572868
  37.2 11.6 %all-to-all-start = ((f32[6,8,256]{2,0,1:T(8,128)}), f32[6,8,256]{2,0,1:T(8,128)S(1)}, u32[]{:S(2)}, u32[]{:S(2)}) async-start(f32[6,8,256]{2,0,1:T(8,128)} %copy.26), calls=%async_computation | async-start | bytes 131072 | tf_op jit(solution)/shard_map/all_to_all | solution.py:203
  77.8 9.9 %copy-start.3 = (bf16[1,512,6]{1,2,0:T(8,128)(2,1)S(1)}, bf16[1,512,6]{1,2,0:T(8,128)(2,1)}, u32[]{:S(2)}) copy-start(bf16[1,512,6]{1,2,0:T(8,128)(2,1)} %param.17) | copy-start | bytes 18436
  87.7 3.5 copy-start.1
  91.1 8.9 %copy-start.2 = (s32[1,1,1024,1]{2,3,1,0:T(1,128)S(1)}, s32[1,1,1024,1]{2,3,1,0:T(1,128)}, u32[]{:S(2)}) copy-start(s32[1,1,1024,1]{2,3,1,0:T(1,128)} %param.12) | copy-start | bytes 12292
  96.4 29.3 %copy-start.4 = (f32[3,2,2,256]{3,2,1,0:T(2,128)S(1)}, f32[3,2,2,256]{3,2,1,0:T(2,128)}, u32[]{:S(2)}) copy-start(f32[3,2,2,256]{3,2,1,0:T(2,128)} %param.11) | copy-start | bytes 36868
  96.4 16.0 %all-to-all-start.2 = ((f32[42,8,256]{2,0,1:T(8,128)}), f32[42,8,256]{2,0,1:T(8,128)S(1)}, u32[]{:S(2)}, u32[]{:S(2)}) async-start(f32[42,8,256]{2,0,1:T(8,128)} %copy.27), calls=%async_computation.2 | async-start | bytes 786432 | tf_op jit(solution)/shard_map/all_to_all | solution.py:217
  116.0 6.6 %collective-permute-start.4 = (f32[42,1,2,256]{3,2,1,0:T(2,128)S(1)}, f32[42,1,2,256]{3,2,1,0:T(2,128)S(1)}, u32[]{:S(2)}, u32[]{:S(2)}) collective-permute-start(f32[42,1,2,256]{3,2,1,0:T(2,128)S(1)} %slice.1305), channel_id=1, source_target_pairs={{0,8},{8,16},{16,24},{1,9},{9,17},{17,25},{2,10},{10,18},{18,26},{... | collective-permute-start | bytes 258056 | tf_op jit(solution)/shard_map/ppermute | solution.py:33
  122.8 2.3 collective-permute-start.5
  126.0 5.6 %collective-permute-start.6 = (f32[3,1,2,256]{3,2,1,0:T(2,128)S(1)}, f32[3,1,2,256]{3,2,1,0:T(2,128)S(1)}, u32[]{:S(2)}, u32[]{:S(2)}) collective-permute-start(f32[3,1,2,256]{3,2,1,0:T(2,128)S(1)} %get-tuple-element.269), channel_id=1, source_target_pairs={{0,8},{8,16},{16,24},{1,9},{9,17},{17,25},{2,10},{10,18},{18,26},{... | collective-permute-start | bytes 18440 | tf_op jit(solution)/shard_map/ppermute | solution.py:22
  130.3 6.8 %collective-permute-start.7 = (f32[3,1,2,256]{3,2,1,0:T(2,128)S(1)}, f32[3,1,2,256]{3,2,1,0:T(2,128)S(1)}, u32[]{:S(2)}, u32[]{:S(2)}) collective-permute-start(f32[3,1,2,256]{3,2,1,0:T(2,128)S(1)} %get-tuple-element.270), channel_id=1, source_target_pairs={{8,0},{16,8},{24,16},{9,1},{17,9},{25,17},{10,2},{18,10},{26,18},{... | collective-permute-start | bytes 18440 | tf_op jit(solution)/shard_map/ppermute | solution.py:25
  137.1 3.5 collective-permute-start.8
  139.2 6.1 %collective-permute-start.9 = (f32[3,4,1,256]{3,2,1,0:T(1,128)S(1)}, f32[3,4,1,256]{3,2,1,0:T(1,128)S(1)}, u32[]{:S(2)}, u32[]{:S(2)}) collective-permute-start(f32[3,4,1,256]{3,2,1,0:T(1,128)S(1)} %get-tuple-element.234), channel_id=1, source_target_pairs={{1,0},{2,1},{3,2},{4,3},{5,4},{6,5},{7,6},{9,8},{10,9},{11,10},{12... | collective-permute-start | bytes 36872 | tf_op jit(solution)/shard_map/ppermute | solution.py:25
  176.4 3.0 collective-permute-start.10
  178.1 6.7 %collective-permute-start.11 = (f32[3,1,2,256]{3,2,1,0:T(2,128)S(1)}, f32[3,1,2,256]{3,2,1,0:T(2,128)S(1)}, u32[]{:S(2)}, u32[]{:S(2)}) collective-permute-start(f32[3,1,2,256]{3,2,1,0:T(2,128)S(1)} %get-tuple-element.268), channel_id=1, source_target_pairs={{8,0},{16,8},{24,16},{9,1},{17,9},{25,17},{10,2},{18,10},{26,18},{... | collective-permute-start | bytes 18440 | tf_op jit(solution)/shard_map/ppermute | solution.py:25
  184.8 2.6 collective-permute-start.12
  186.1 3.1 collective-permute-start.13
  222.1 3.0 collective-permute-start.14
  223.7 6.7 %collective-permute-start.15 = (f32[3,1,2,256]{3,2,1,0:T(2,128)S(1)}, f32[3,1,2,256]{3,2,1,0:T(2,128)S(1)}, u32[]{:S(2)}, u32[]{:S(2)}) collective-permute-start(f32[3,1,2,256]{3,2,1,0:T(2,128)S(1)} %get-tuple-element.266), channel_id=1, source_target_pairs={{8,0},{16,8},{24,16},{9,1},{17,9},{25,17},{10,2},{18,10},{26,18},{... | collective-permute-start | bytes 18440 | tf_op jit(solution)/shard_map/ppermute | solution.py:25
  230.4 2.6 collective-permute-start.16
  231.7 3.1 collective-permute-start.17
  267.0 3.0 collective-permute-start.18
  268.6 6.7 %collective-permute-start.19 = (f32[3,1,2,256]{3,2,1,0:T(2,128)S(1)}, f32[3,1,2,256]{3,2,1,0:T(2,128)S(1)}, u32[]{:S(2)}, u32[]{:S(2)}) collective-permute-start(f32[3,1,2,256]{3,2,1,0:T(2,128)S(1)} %get-tuple-element.264), channel_id=1, source_target_pairs={{8,0},{16,8},{24,16},{9,1},{17,9},{25,17},{10,2},{18,10},{26,18},{... | collective-permute-start | bytes 18440 | tf_op jit(solution)/shard_map/ppermute | solution.py:25
  275.4 2.6 collective-permute-start.20
  276.7 3.1 collective-permute-start.21
  312.4 3.0 collective-permute-start.22
  314.0 6.7 %collective-permute-start.23 = (f32[3,1,2,256]{3,2,1,0:T(2,128)S(1)}, f32[3,1,2,256]{3,2,1,0:T(2,128)S(1)}, u32[]{:S(2)}, u32[]{:S(2)}) collective-permute-start(f32[3,1,2,256]{3,2,1,0:T(2,128)S(1)} %get-tuple-element.262), channel_id=1, source_target_pairs={{8,0},{16,8},{24,16},{9,1},{17,9},{25,17},{10,2},{18,10},{26,18},{... | collective-permute-start | bytes 18440 | tf_op jit(solution)/shard_map/ppermute | solution.py:25
  320.8 2.6 collective-permute-start.24
  322.1 3.1 collective-permute-start.25
